TPU v7x, 256 devices: a whole 4x4x8 slice. The times are simulated.
256 devices in a mesh: gx: 16 (over z_hi, y, core), gy: 16 (over x, z_lo).
Axes of the slice: x: 4, y: 4, z: 8 (z_hi: 2, z_lo: 4; z = z_hi * 4 + z_lo), core: 2. Of those that a mesh axis runs over, the one named last changes fastest.
Arguments:
- adjoint_rhs: float32 [32, 16, 768, 128], P('gx', 'gy'), may hold values from -6 to 6
- local_inverse: bfloat16 [32, 16, 1024, 768], P('gx', 'gy')
- local_operator: bfloat16 [32, 16, 1024, 768], P('gx', 'gy')
- spill_rows: int32 [32, 16, 4, 64], P('gx', 'gy'), may hold values from 0 to 767, as said below
- coarse_basis: bfloat16 [32, 16, 64, 768], P('gx', 'gy'), may hold values from -3 to 3
- coarse_ids: int32 [32, 16, 64], P('gx', 'gy'), may hold values from 0 to 1023
- coarse_inverse: bfloat16 [1024, 1024], P(('gx', 'gy')), may hold values from -0.00030517578 to 0.00030517578
Outputs:
- adjoint_solution: float32 [32, 16, 768, 128], P('gx', 'gy')
- residual: float32 [32, 16, 768, 128], P('gx', 'gy')
Inputs may be any that keep to these rules, and one draw needn't show every extreme that they name: Each list of spill_rows holds 64 distinct rows. `coarse_ids`: A coarse function may be listed more than once for a subdomain.
All inputs are finite; a program needn't handle non-finite values.
Results may differ from a plain program's by a relative error of at most 0.0041.
Values may be sent and summed in bfloat16 or wider, within the bound.
A program may use at most 64 MiB of HBM per device.

v0:
```python
import jax
import jax.numpy as jnp
from jax import lax
from jax.sharding import PartitionSpec as P


def with_halo(block, sides, width):
    for axis, dim in sides:
        count = lax.axis_size(axis)
        forward = [(i, i + 1) for i in range(count - 1)]
        backward = [(target, source) for source, target in forward]
        low = lax.ppermute(
            lax.slice_in_dim(block, block.shape[dim] - width, None, axis=dim), axis, forward
        )
        high = lax.ppermute(lax.slice_in_dim(block, 0, width, axis=dim), axis, backward)
        block = jnp.concatenate([low, block, high], axis=dim)
    return block


def add_rows(owned_rows, indices, values):
    return owned_rows.at[indices].add(values)


def spread(extended, indices):
    sub_count = extended.shape[0]
    group_rows = indices.shape[1] // 4
    owned_count = extended.shape[1] - 4 * group_rows
    owned_rows = extended[:, :owned_count]
    groups = extended[:, owned_count:].reshape(sub_count, 4, group_rows, extended.shape[2])
    outward = jnp.stack([groups[0, 0], groups[sub_count - 1, 1]])
    across = with_halo(outward, (("gx", 0),), 1)
    from_west = jnp.concatenate([across[0][None], groups[:-1, 1]], 0)
    from_east = jnp.concatenate([groups[1:, 0], across[3][None]], 0)
    vertical = jnp.stack([groups[:, 2], groups[:, 3]])
    beside = with_halo(vertical, (("gy", 0),), 1)
    received = jnp.stack([from_west, from_east, beside[0], beside[3]], 1).reshape(
        sub_count, 4 * group_rows, extended.shape[2]
    )
    return jax.vmap(add_rows)(owned_rows, indices, received)


def body(
    adjoint_rhs, local_inverse, local_operator, spill_rows, coarse_basis, coarse_ids, coarse_inverse
):
    highest = lax.Precision.HIGHEST
    contract_first = (((0,), (0,)), ((), ()))
    residual = adjoint_rhs[:, 0]
    inverses = local_inverse[:, 0]
    operators = local_operator[:, 0]
    indices = spill_rows[:, 0].reshape(spill_rows.shape[0], -1)
    basis_rows = coarse_basis[:, 0].astype(jnp.float32)
    sub_count = coarse_ids.shape[0]
    functions = coarse_ids.shape[2]
    coarse_order = coarse_inverse.shape[1]
    flat_ids = coarse_ids[:, 0].reshape(-1)
    one_hot = (flat_ids[None, :] == jnp.arange(coarse_order, dtype=jnp.int32)[:, None]).astype(
        jnp.float32
    )
    terms = jnp.einsum("skn,snr->skr", basis_rows, residual, precision=highest)
    local_sums = jnp.dot(
        one_hot, terms.reshape(sub_count * functions, terms.shape[2]), precision=highest
    )
    shares = lax.psum_scatter(local_sums, ("gx", "gy"), scatter_dimension=0, tiled=True)
    partial_sol = lax.dot_general(
        coarse_inverse,
        shares.astype(jnp.bfloat16),
        contract_first,
        preferred_element_type=jnp.float32,
    )
    coarse_sol = lax.psum(partial_sol, ("gx", "gy"))
    local_sol = jnp.einsum(
        "sln,snr->slr", inverses, residual.astype(jnp.bfloat16), preferred_element_type=jnp.float32
    )
    picked = jnp.dot(one_hot.T, coarse_sol, precision=highest).reshape(
        sub_count, functions, coarse_sol.shape[1]
    )
    coarse_part = jnp.einsum("skn,skr->snr", basis_rows, picked, precision=highest)
    correction = spread(local_sol, indices) + coarse_part
    image = jnp.einsum(
        "sln,snr->slr",
        operators,
        correction.astype(jnp.bfloat16),
        preferred_element_type=jnp.float32,
    )
    residual = residual - spread(image, indices)
    return (correction[:, None], residual[:, None])


def solution(mesh):
    in_specs = (
        P("gx", "gy", None, None),
        P("gx", "gy", None, None),
        P("gx", "gy", None, None),
        P("gx", "gy", None, None),
        P("gx", "gy", None, None),
        P("gx", "gy", None),
        P(("gx", "gy"), None),
    )
    out_specs = (P("gx", "gy", None, None), P("gx", "gy", None, None))
    return jax.shard_map(body, mesh=mesh, in_specs=in_specs, out_specs=out_specs, check_vma=False)
```

profile of v0, /device:TPU:226, one launch (start us, length us, event | category | flops | bytes accessed | tf_op | source)
XLA Modules:
  0.0 501.2 jit_solution(17594343954247628550)
XLA Ops:
  7.7 1.6 reduce.3
  9.5 1.6 fusion.8
  12.3 75.3 %all-reduce.5 = bf16[1024,128]{1,0:T(8,128)(2,1)S(1)} all-reduce(f32[1024,128]{1,0:T(8,128)} %fusion.12), channel_id=2, replica_groups=mesh['gx'=16,'gy'=16] {'gx','gy'}, use_global_device_ids=true, to_apply=%region_0.0.clone | all-reduce | flops 131072 | bytes 786432
  87.6 1.8 convolution_bitcast_fusion.1
  89.4 2.1 fusion.2
  93.2 3.7 collective-permute-start
  96.8 7.9 %collective-permute-start.1 = (f32[1,64,128]{2,1,0:T(8,128)}, f32[1,64,128]{2,1,0:T(8,128)S(1)}, u32[]{:S(2)}, u32[]{:S(2)}) collective-permute-start(f32[1,64,128]{2,1,0:T(8,128)} %get-tuple-element.15), channel_id=1, source_target_pairs={{16,0},{32,16},{48,32},{64,48},{80,64},{96,80},{112,96},{128,112},... | collective-permute-start | bytes 98312 | tf_op jit(solution)/shard_map/ppermute | solution.py:15
  104.8 5.4 %collective-permute-start.2 = (f32[1,2,64,128]{3,2,1,0:T(8,128)S(1)}, f32[1,2,64,128]{3,2,1,0:T(8,128)S(1)}, u32[]{:S(2)}, u32[]{:S(2)}) collective-permute-start(f32[1,2,64,128]{3,2,1,0:T(8,128)S(1)} %get-tuple-element.18), channel_id=1, source_target_pairs={{0,1},{1,2},{2,3},{3,4},{4,5},{5,6},{6,7},{7,8},{8,9},{9,10},{10,1... | collective-permute-start | bytes 196616 | tf_op jit(solution)/shard_map/ppermute | solution.py:12
  110.1 1.9 collective-permute-start.3
  112.2 6.8 %collective-permute-done.3 = f32[1,2,64,128]{3,2,1,0:T(8,128)S(1)} collective-permute-done((f32[1,2,64,128]{3,2,1,0:T(8,128)S(1)}, f32[1,2,64,128]{3,2,1,0:T(8,128)S(1)}, u32[]{:S(2)}, u32[]{:S(2)}) %collective-permute-start.3) | collective-permute-done | bytes 65568 | tf_op jit(solution)/shard_map/ppermute | solution.py:15
  119.1 224.2 %all-reduce.4.cloned.1.call-done = f32[1024,128]{0,1:T(8,128)} async-done(((f32[1024,128]{0,1:T(8,128)}), f32[1024,128]{0,1:T(8,128)}) %all-reduce.4.cloned.1.call-update) | async-done | bytes 524304 | tf_op jit(solution)/shard_map/psum | solution.py:70
  343.3 1.5 fusion.14
  344.9 2.7 fusion.7
  347.5 54.2 %scatter_fusion = f32[2,768,128]{2,1,0:T(8,128)} fusion(f32[2,768,128]{2,1,0:T(8,128)} %fusion.7, s32[512]{0:T(512)S(1)} %bitcast.99, f32[512,128]{1,0:T(8,128)S(1)} %bitcast.102), kind=kCustom, calls=%fused_computation | custom fusion | flops 65536 | bytes 790528 | tf_op jit(solution)/shard_map/vmap()/scatter-add | solution.py:21
  401.7 3.3 fusion.4
  408.5 3.2 collective-permute-start.4
  412.3 2.1 slice.76
  414.4 2.3 copy.41
  416.7 8.3 %collective-permute-start.5 = (f32[1,64,128]{2,1,0:T(8,128)S(1)}, f32[1,64,128]{2,1,0:T(8,128)S(1)}, u32[]{:S(2)}, u32[]{:S(2)}) collective-permute-start(f32[1,64,128]{2,1,0:T(8,128)S(1)} %copy-done.4), channel_id=1, source_target_pairs={{16,0},{32,16},{48,32},{64,48},{80,64},{96,80},{112,96},{128,112},... | collective-permute-start | bytes 98312 | tf_op jit(solution)/shard_map/ppermute | solution.py:15
  425.1 6.7 %collective-permute-start.6 = (f32[1,2,64,128]{3,2,1,0:T(8,128)S(1)}, f32[1,2,64,128]{3,2,1,0:T(8,128)S(1)}, u32[]{:S(2)}, u32[]{:S(2)}) collective-permute-start(f32[1,2,64,128]{3,2,1,0:T(8,128)S(1)} %copy-done.3), channel_id=1, source_target_pairs={{0,1},{1,2},{2,3},{3,4},{4,5},{5,6},{6,7},{7,8},{8,9},{9,10},{10,1... | collective-permute-start | bytes 196616 | tf_op jit(solution)/shard_map/ppermute | solution.py:12
  431.8 1.9 collective-permute-start.7
  434.5 6.1 %collective-permute-done.7 = f32[1,2,64,128]{3,2,1,0:T(8,128)S(1)} collective-permute-done((f32[1,2,64,128]{3,2,1,0:T(8,128)S(1)}, f32[1,2,64,128]{3,2,1,0:T(8,128)S(1)}, u32[]{:S(2)}, u32[]{:S(2)}) %collective-permute-start.7) | collective-permute-done | bytes 65568 | tf_op jit(solution)/shard_map/ppermute | solution.py:15
  440.7 51.3 %scatter_fusion.1 = f32[2,768,128]{2,1,0:T(8,128)} fusion(f32[2,768,128]{2,1,0:T(8,128)} %copy.41, s32[512]{0:T(512)S(1)} %bitcast.100, f32[512,128]{1,0:T(8,128)S(1)} %bitcast.103), kind=kCustom, calls=%fused_computation.1 | custom fusion | flops 65536 | bytes 790528 | tf_op jit(solution)/shard_map/vmap()/scatter-add | solution.py:21
  492.0 2.3 fusion.10
  (41 shorter events, 8.5 us)
Async XLA Ops:
  7.2 82.2 %copy-start = (bf16[2,1,1024,768]{3,2,1,0:T(8,128)(2,1)S(1)}, bf16[2,1,1024,768]{3,2,1,0:T(8,128)(2,1)}, u32[]{:S(2)}) copy-start(bf16[2,1,1024,768]{3,2,1,0:T(8,128)(2,1)} %param.8) | copy-start | bytes 9437188
  7.2 336.2 %all-reduce.4.cloned.1.call-start = ((), (), s32[]{:S(2)}) async-start(), calls=%async_computation | async-start | bytes 1048576 | tf_op jit(solution)/shard_map/psum | solution.py:70
  89.4 22.7 %copy-start.5 = (s32[2,1,4,64]{3,2,1,0:T(4,128)S(1)}, s32[2,1,4,64]{3,2,1,0:T(4,128)}, u32[]{:S(2)}) copy-start(s32[2,1,4,64]{3,2,1,0:T(4,128)} %param.10) | copy-start | bytes 6148
  91.5 1.0 copy-start.1
  93.2 19.0 %collective-permute-start = (f32[1,64,128]{2,1,0:T(8,128)}, f32[1,64,128]{2,1,0:T(8,128)S(1)}, u32[]{:S(2)}, u32[]{:S(2)}) collective-permute-start(f32[1,64,128]{2,1,0:T(8,128)} %get-tuple-element.14), channel_id=1, source_target_pairs={{0,16},{16,32},{32,48},{48,64},{64,80},{80,96},{96,112},{112,128},... | collective-permute-start | bytes 98312 | tf_op jit(solution)/shard_map/ppermute | solution.py:12
  96.8 15.4 %collective-permute-start.1 = (f32[1,64,128]{2,1,0:T(8,128)}, f32[1,64,128]{2,1,0:T(8,128)S(1)}, u32[]{:S(2)}, u32[]{:S(2)}) collective-permute-start(f32[1,64,128]{2,1,0:T(8,128)} %get-tuple-element.15), channel_id=1, source_target_pairs={{16,0},{32,16},{48,32},{64,48},{80,64},{96,80},{112,96},{128,112},... | collective-permute-start | bytes 98312 | tf_op jit(solution)/shard_map/ppermute | solution.py:15
  104.8 7.5 %collective-permute-start.2 = (f32[1,2,64,128]{3,2,1,0:T(8,128)S(1)}, f32[1,2,64,128]{3,2,1,0:T(8,128)S(1)}, u32[]{:S(2)}, u32[]{:S(2)}) collective-permute-start(f32[1,2,64,128]{3,2,1,0:T(8,128)S(1)} %get-tuple-element.18), channel_id=1, source_target_pairs={{0,1},{1,2},{2,3},{3,4},{4,5},{5,6},{6,7},{7,8},{8,9},{9,10},{10,1... | collective-permute-start | bytes 196616 | tf_op jit(solution)/shard_map/ppermute | solution.py:12
  110.1 8.9 %collective-permute-start.3 = (f32[1,2,64,128]{3,2,1,0:T(8,128)S(1)}, f32[1,2,64,128]{3,2,1,0:T(8,128)S(1)}, u32[]{:S(2)}, u32[]{:S(2)}) collective-permute-start(f32[1,2,64,128]{3,2,1,0:T(8,128)S(1)} %get-tuple-element.19), channel_id=1, source_target_pairs={{1,0},{2,1},{3,2},{4,3},{5,4},{6,5},{7,6},{8,7},{9,8},{10,9},{11,1... | collective-permute-start | bytes 196616 | tf_op jit(solution)/shard_map/ppermute | solution.py:15
  405.0 1.0 copy-start.2
  408.5 25.3 %collective-permute-start.4 = (f32[1,64,128]{2,1,0:T(8,128)}, f32[1,64,128]{2,1,0:T(8,128)}, u32[]{:S(2)}, u32[]{:S(2)}) collective-permute-start(f32[1,64,128]{2,1,0:T(8,128)} %get-tuple-element.8), channel_id=1, source_target_pairs={{0,16},{16,32},{32,48},{48,64},{64,80},{80,96},{96,112},{112,128},... | collective-permute-start | bytes 98312 | tf_op jit(solution)/shard_map/ppermute | solution.py:12
  412.3 4.4 copy-start.4
  412.3 12.8 %copy-start.3 = (f32[1,2,64,128]{3,2,1,0:T(8,128)S(1)}, f32[1,2,64,128]{3,2,1,0:T(8,128)}, u32[]{:S(2)}) copy-start(f32[1,2,64,128]{3,2,1,0:T(8,128)} %get-tuple-element.12) | copy-start | bytes 196612
  416.7 17.8 %collective-permute-start.5 = (f32[1,64,128]{2,1,0:T(8,128)S(1)}, f32[1,64,128]{2,1,0:T(8,128)S(1)}, u32[]{:S(2)}, u32[]{:S(2)}) collective-permute-start(f32[1,64,128]{2,1,0:T(8,128)S(1)} %copy-done.4), channel_id=1, source_target_pairs={{16,0},{32,16},{48,32},{64,48},{80,64},{96,80},{112,96},{128,112},... | collective-permute-start | bytes 98312 | tf_op jit(solution)/shard_map/ppermute | solution.py:15
  425.1 9.5 %collective-permute-start.6 = (f32[1,2,64,128]{3,2,1,0:T(8,128)S(1)}, f32[1,2,64,128]{3,2,1,0:T(8,128)S(1)}, u32[]{:S(2)}, u32[]{:S(2)}) collective-permute-start(f32[1,2,64,128]{3,2,1,0:T(8,128)S(1)} %copy-done.3), channel_id=1, source_target_pairs={{0,1},{1,2},{2,3},{3,4},{4,5},{5,6},{6,7},{7,8},{8,9},{9,10},{10,1... | collective-permute-start | bytes 196616 | tf_op jit(solution)/shard_map/ppermute | solution.py:12
  431.8 8.9 %collective-permute-start.7 = (f32[1,2,64,128]{3,2,1,0:T(8,128)S(1)}, f32[1,2,64,128]{3,2,1,0:T(8,128)S(1)}, u32[]{:S(2)}, u32[]{:S(2)}) collective-permute-start(f32[1,2,64,128]{3,2,1,0:T(8,128)S(1)} %get-tuple-element.13), channel_id=1, source_target_pairs={{1,0},{2,1},{3,2},{4,3},{5,4},{6,5},{7,6},{8,7},{9,8},{10,9},{11,1... | collective-permute-start | bytes 196616 | tf_op jit(solution)/shard_map/ppermute | solution.py:15
Sparse Core Ops, SparseCore 0:
  89.5 253.7 all-reduce.3
where the time goes:
time: 504 us; the launch traced here: 501 us
  waiting for transfers between devices  237 us (47%)
  other arithmetic  110 us (22%)
  blocking collectives  75.3 us (15%)
  starting transfers between devices  39.1 us (8%)
  between operations  14.3 us (3%)
  matrix products  14.2 us (3%)
  local copies, waits for them, and re-layouts  10.8 us (2%)
    psum x1, waiting for transfers between devices, body(): coarse_sol = lax.psum(partial_sol, ('gx', 'gy'))  224 us
    scatter-add x2, other arithmetic, add_rows(): return owned_rows.at[indices].add(values)  105 us
    unnamed x1, blocking collectives  75.3 us
    ppermute x4, starting transfers between devices, with_halo(): lax.ppermute(lax.slice_in_dim(block, 0, width, axis=dim), axis, backward)  20.1 us
    ppermute x4, starting transfers between devices, with_halo(): lax.ppermute(lax.slice_in_dim(block, block.shape[dim] - width, None, axis...  19 us
    ppermute x4, waiting for transfers between devices, with_halo(): lax.ppermute(lax.slice_in_dim(block, 0, width, axis=dim), axis, backward)  12.9 us
  transfers between devices with their start and end apart: 9, of which 3 were waited for; matrix products, arithmetic and copies ran while one was open for 2% of the time, Pallas kernels for 0%

commit v1 on v0

--- a/solution.py
+++ b/solution.py
@@ -67,7 +67,7 @@
         contract_first,
         preferred_element_type=jnp.float32,
     )
-    coarse_sol = lax.psum(partial_sol, ("gx", "gy"))
+    coarse_sol = lax.psum(lax.psum(partial_sol, "gy"), "gx")
     local_sol = jnp.einsum(
         "sln,snr->slr", inverses, residual.astype(jnp.bfloat16), preferred_element_type=jnp.float32
     )

time: 504 us -> 592 us (1.17)
  waiting for transfers between devices: 237 us -> 326 us
    psum x1 -> x2, waiting for transfers between devices: 224 us -> 320 us  [body(): coarse_sol = lax.psum(lax.psum(partial_sol, 'gy'), 'gx')]
    ppermute x4, waiting for transfers between devices: 12.9 us -> 6.14 us  [with_halo(): lax.ppermute(lax.slice_in_dim(block, 0, width, axis=dim), axis, backward)]
  transfers between devices with their start and end apart: 9 -> 10, of which waited for: 3 -> 3; matrix products, arithmetic and copies ran while one was open for 2% -> 1% of each run, Pallas kernels for 0% -> 0%
where the time goes in v1:
time: 592 us; the launch traced here: 589 us
  waiting for transfers between devices  326 us (55%)
  other arithmetic  110 us (19%)
  blocking collectives  75.3 us (13%)
  starting transfers between devices  38.2 us (6%)
  between operations  14.3 us (2%)
  matrix products  14.2 us (2%)
  local copies, waits for them, and re-layouts  10.8 us (2%)
    psum x2, waiting for transfers between devices, body(): coarse_sol = lax.psum(lax.psum(partial_sol, 'gy'), 'gx')  320 us
    scatter-add x2, other arithmetic, add_rows(): return owned_rows.at[indices].add(values)  105 us
    unnamed x1, blocking collectives  75.3 us
    ppermute x4, starting transfers between devices, with_halo(): lax.ppermute(lax.slice_in_dim(block, 0, width, axis=dim), axis, backward)  21.4 us
    ppermute x4, starting transfers between devices, with_halo(): lax.ppermute(lax.slice_in_dim(block, block.shape[dim] - width, None, axis...  16.8 us
  transfers between devices with their start and end apart: 10, of which 3 were waited for; matrix products, arithmetic and copies ran while one was open for 1% of the time, Pallas kernels for 0%

profile of v1, /device:TPU:226, one launch (start us, length us, event | category | flops | bytes accessed | tf_op | source)
XLA Modules:
  0.0 589.1 jit_solution(353823025265678290)
XLA Ops:
  7.7 1.6 reduce.3
  9.5 1.6 fusion.8
  12.3 75.3 %all-reduce.8 = bf16[1024,128]{1,0:T(8,128)(2,1)S(1)} all-reduce(f32[1024,128]{1,0:T(8,128)} %fusion.12), channel_id=2, replica_groups=mesh['gx'=16,'gy'=16] {'gx','gy'}, use_global_device_ids=true, to_apply=%region_0.0.clone | all-reduce | flops 131072 | bytes 786432
  87.6 1.8 convolution_bitcast_fusion.1
  89.5 2.1 fusion.2
  93.2 3.7 collective-permute-start
  96.9 7.9 %collective-permute-start.1 = (f32[1,64,128]{2,1,0:T(8,128)}, f32[1,64,128]{2,1,0:T(8,128)S(1)}, u32[]{:S(2)}, u32[]{:S(2)}) collective-permute-start(f32[1,64,128]{2,1,0:T(8,128)} %get-tuple-element.15), channel_id=1, source_target_pairs={{16,0},{32,16},{48,32},{64,48},{80,64},{96,80},{112,96},{128,112},... | collective-permute-start | bytes 98312 | tf_op jit(solution)/shard_map/ppermute | solution.py:15
  104.8 5.4 collective-permute-start.2
  110.2 1.9 collective-permute-start.3
  112.2 132.2 %all-reduce.5.cloned.1.call-done = f32[1024,128]{0,1:T(8,128)} async-done(((f32[1024,128]{0,1:T(8,128)}), f32[1024,128]{0,1:T(8,128)}) %all-reduce.5.cloned.1.call-update) | async-done | bytes 524304 | tf_op jit(solution)/shard_map/psum | solution.py:70
  244.6 187.6 %all-reduce.7.cloned.1.call-done = f32[1024,128]{0,1:T(8,128)} async-done(((f32[1024,128]{0,1:T(8,128)}), f32[1024,128]{0,1:T(8,128)}) %all-reduce.7.cloned.1.call-update) | async-done | bytes 524304 | tf_op jit(solution)/shard_map/psum | solution.py:70
  432.2 1.5 fusion.14
  433.7 2.7 fusion.7
  436.4 54.2 %scatter_fusion = f32[2,768,128]{2,1,0:T(8,128)} fusion(f32[2,768,128]{2,1,0:T(8,128)} %fusion.7, s32[512]{0:T(512)S(1)} %bitcast.99, f32[512,128]{1,0:T(8,128)S(1)} %bitcast.102), kind=kCustom, calls=%fused_computation | custom fusion | flops 65536 | bytes 790528 | tf_op jit(solution)/shard_map/vmap()/scatter-add | solution.py:21
  490.6 3.3 fusion.4
  497.3 1.9 collective-permute-start.4
  499.9 2.1 slice.76
  502.0 2.3 copy.41
  504.3 9.6 %collective-permute-start.5 = (f32[1,64,128]{2,1,0:T(8,128)S(1)}, f32[1,64,128]{2,1,0:T(8,128)S(1)}, u32[]{:S(2)}, u32[]{:S(2)}) collective-permute-start(f32[1,64,128]{2,1,0:T(8,128)S(1)} %copy-done.4), channel_id=1, source_target_pairs={{16,0},{32,16},{48,32},{64,48},{80,64},{96,80},{112,96},{128,112},... | collective-permute-start | bytes 98312 | tf_op jit(solution)/shard_map/ppermute | solution.py:15
  513.9 5.8 collective-permute-start.6
  519.7 1.9 collective-permute-start.7
  522.5 6.1 %collective-permute-done.7 = f32[1,2,64,128]{3,2,1,0:T(8,128)S(1)} collective-permute-done((f32[1,2,64,128]{3,2,1,0:T(8,128)S(1)}, f32[1,2,64,128]{3,2,1,0:T(8,128)S(1)}, u32[]{:S(2)}, u32[]{:S(2)}) %collective-permute-start.7) | collective-permute-done | bytes 65568 | tf_op jit(solution)/shard_map/ppermute | solution.py:15
  528.7 51.3 %scatter_fusion.1 = f32[2,768,128]{2,1,0:T(8,128)} fusion(f32[2,768,128]{2,1,0:T(8,128)} %copy.41, s32[512]{0:T(512)S(1)} %bitcast.100, f32[512,128]{1,0:T(8,128)S(1)} %bitcast.103), kind=kCustom, calls=%fused_computation.1 | custom fusion | flops 65536 | bytes 790528 | tf_op jit(solution)/shard_map/vmap()/scatter-add | solution.py:21
  579.9 2.3 fusion.10
  (44 shorter events, 8.5 us)
Async XLA Ops:
  7.2 82.3 %copy-start = (bf16[2,1,1024,768]{3,2,1,0:T(8,128)(2,1)S(1)}, bf16[2,1,1024,768]{3,2,1,0:T(8,128)(2,1)}, u32[]{:S(2)}) copy-start(bf16[2,1,1024,768]{3,2,1,0:T(8,128)(2,1)} %param.8) | copy-start | bytes 9437188
  7.2 237.2 %all-reduce.5.cloned.1.call-start = ((), (), s32[]{:S(2)}) async-start(), calls=%async_computation | async-start | bytes 1048576 | tf_op jit(solution)/shard_map/psum | solution.py:70
  89.4 22.7 %copy-start.5 = (s32[2,1,4,64]{3,2,1,0:T(4,128)S(1)}, s32[2,1,4,64]{3,2,1,0:T(4,128)}, u32[]{:S(2)}) copy-start(s32[2,1,4,64]{3,2,1,0:T(4,128)} %param.10) | copy-start | bytes 6148
  89.4 342.8 %all-reduce.7.cloned.1.call-start = ((), (), s32[]{:S(2)}) async-start(), calls=%async_computation.1 | async-start | bytes 1048576 | tf_op jit(solution)/shard_map/psum | solution.py:70
  91.6 1.0 copy-start.1
  93.2 151.3 %collective-permute-start = (f32[1,64,128]{2,1,0:T(8,128)}, f32[1,64,128]{2,1,0:T(8,128)S(1)}, u32[]{:S(2)}, u32[]{:S(2)}) collective-permute-start(f32[1,64,128]{2,1,0:T(8,128)} %get-tuple-element.14), channel_id=1, source_target_pairs={{0,16},{16,32},{32,48},{48,64},{64,80},{80,96},{96,112},{112,128},... | collective-permute-start | bytes 98312 | tf_op jit(solution)/shard_map/ppermute | solution.py:12
  96.9 147.6 %collective-permute-start.1 = (f32[1,64,128]{2,1,0:T(8,128)}, f32[1,64,128]{2,1,0:T(8,128)S(1)}, u32[]{:S(2)}, u32[]{:S(2)}) collective-permute-start(f32[1,64,128]{2,1,0:T(8,128)} %get-tuple-element.15), channel_id=1, source_target_pairs={{16,0},{32,16},{48,32},{64,48},{80,64},{96,80},{112,96},{128,112},... | collective-permute-start | bytes 98312 | tf_op jit(solution)/shard_map/ppermute | solution.py:15
  104.8 139.7 %collective-permute-start.2 = (f32[1,2,64,128]{3,2,1,0:T(8,128)S(1)}, f32[1,2,64,128]{3,2,1,0:T(8,128)S(1)}, u32[]{:S(2)}, u32[]{:S(2)}) collective-permute-start(f32[1,2,64,128]{3,2,1,0:T(8,128)S(1)} %get-tuple-element.18), channel_id=1, source_target_pairs={{0,1},{1,2},{2,3},{3,4},{4,5},{5,6},{6,7},{7,8},{8,9},{9,10},{10,1... | collective-permute-start | bytes 196616 | tf_op jit(solution)/shard_map/ppermute | solution.py:12
  110.2 134.3 %collective-permute-start.3 = (f32[1,2,64,128]{3,2,1,0:T(8,128)S(1)}, f32[1,2,64,128]{3,2,1,0:T(8,128)S(1)}, u32[]{:S(2)}, u32[]{:S(2)}) collective-permute-start(f32[1,2,64,128]{3,2,1,0:T(8,128)S(1)} %get-tuple-element.19), channel_id=1, source_target_pairs={{1,0},{2,1},{3,2},{4,3},{5,4},{6,5},{7,6},{8,7},{9,8},{10,9},{11,1... | collective-permute-start | bytes 196616 | tf_op jit(solution)/shard_map/ppermute | solution.py:15
  493.9 1.0 copy-start.2
  497.3 24.4 %collective-permute-start.4 = (f32[1,64,128]{2,1,0:T(8,128)}, f32[1,64,128]{2,1,0:T(8,128)}, u32[]{:S(2)}, u32[]{:S(2)}) collective-permute-start(f32[1,64,128]{2,1,0:T(8,128)} %get-tuple-element.8), channel_id=1, source_target_pairs={{0,16},{16,32},{32,48},{48,64},{64,80},{80,96},{96,112},{112,128},... | collective-permute-start | bytes 98312 | tf_op jit(solution)/shard_map/ppermute | solution.py:12
  499.9 4.4 copy-start.4
  499.9 14.1 %copy-start.3 = (f32[1,2,64,128]{3,2,1,0:T(8,128)S(1)}, f32[1,2,64,128]{3,2,1,0:T(8,128)}, u32[]{:S(2)}) copy-start(f32[1,2,64,128]{3,2,1,0:T(8,128)} %get-tuple-element.12) | copy-start | bytes 196612
  504.3 18.2 %collective-permute-start.5 = (f32[1,64,128]{2,1,0:T(8,128)S(1)}, f32[1,64,128]{2,1,0:T(8,128)S(1)}, u32[]{:S(2)}, u32[]{:S(2)}) collective-permute-start(f32[1,64,128]{2,1,0:T(8,128)S(1)} %copy-done.4), channel_id=1, source_target_pairs={{16,0},{32,16},{48,32},{64,48},{80,64},{96,80},{112,96},{128,112},... | collective-permute-start | bytes 98312 | tf_op jit(solution)/shard_map/ppermute | solution.py:15
  513.9 8.5 %collective-permute-start.6 = (f32[1,2,64,128]{3,2,1,0:T(8,128)S(1)}, f32[1,2,64,128]{3,2,1,0:T(8,128)S(1)}, u32[]{:S(2)}, u32[]{:S(2)}) collective-permute-start(f32[1,2,64,128]{3,2,1,0:T(8,128)S(1)} %copy-done.3), channel_id=1, source_target_pairs={{0,1},{1,2},{2,3},{3,4},{4,5},{5,6},{6,7},{7,8},{8,9},{9,10},{10,1... | collective-permute-start | bytes 196616 | tf_op jit(solution)/shard_map/ppermute | solution.py:12
  519.7 8.9 %collective-permute-start.7 = (f32[1,2,64,128]{3,2,1,0:T(8,128)S(1)}, f32[1,2,64,128]{3,2,1,0:T(8,128)S(1)}, u32[]{:S(2)}, u32[]{:S(2)}) collective-permute-start(f32[1,2,64,128]{3,2,1,0:T(8,128)S(1)} %get-tuple-element.13), channel_id=1, source_target_pairs={{1,0},{2,1},{3,2},{4,3},{5,4},{6,5},{7,6},{8,7},{9,8},{10,9},{11,1... | collective-permute-start | bytes 196616 | tf_op jit(solution)/shard_map/ppermute | solution.py:15
Sparse Core Ops, SparseCore 0:
  89.5 154.8 all-reduce.4
  247.0 185.1 all-reduce.6
